TPU v7x, 256 devices: a whole 4x4x8 slice. The times are simulated.
256 devices in a mesh: freq: 32 (over x, y, core), mode: 8 (over z).
Axes of the slice: x: 4, y: 4, z: 8, core: 2. Of those that a mesh axis runs over, the one named last changes fastest.
Arguments:
- excitation: bfloat16 [16, 2, 1024, 2048], P(None, None, 'freq', 'mode'), may hold values from -6 to 6
- coupling: bfloat16 [3, 32, 2, 2048, 2048], P(None, 'freq', None, 'mode'), may hold values from -3 to 3, as said below
- wavenumber: float32 [1024, 2048], P('freq', 'mode'), may hold values from 0.02 to 0.2
- mode_counts: int32 [1024], P('freq'), may hold values from 128 to 2048, as said below
- seg_steps: int32 [3], replicated, may hold values from 8 to 64
- shapes: bfloat16 [32, 2048, 512], P('freq'), may hold values from -0.125 to 0.125
- spectrum: float32 [2, 1024], P(None, 'freq'), may hold values from -6 to 6
Outputs:
- traces: float32 [16, 512, 4096], P('mode', 'freq')
Inputs may be any that keep to these rules, and one draw needn't show every extreme that they name: `mode_counts`: each count is a multiple of 128; counts tend to rise with frequency; the first frequency has 128 modes and the last has all 2048. `coupling`: the real part of each matrix is near the identity on its diagonal; all entries are independent otherwise.
All inputs are finite; a program needn't handle non-finite values.
Results may differ from a plain program's by a relative error of at most 0.015.
Values may be sent and summed in bfloat16 or wider, within the bound.
No kernel may reach another device: no remote copies, remote signals or barrier semaphores. Data moves between devices by JAX's collectives and lax.ppermute only.
A program may use at most 128 MiB of HBM per device.

v0:
```python
import math
import jax
import jax.numpy as jnp
from jax import lax
from jax.sharding import PartitionSpec as P

NT = 4096


def make_table(count, offset_bin):
    freq_index = jnp.arange(count, dtype=jnp.int32)
    sample = jnp.arange(NT, dtype=jnp.int32)
    phase_step = (freq_index[:, None] + offset_bin) * sample[None, :] % NT
    angles = phase_step.astype(jnp.float32) * (2.0 * math.pi / NT)
    return jnp.stack([jnp.cos(angles), -jnp.sin(angles)], axis=0).astype(jnp.bfloat16)


def shards(excitation, coupling, wavenumber, mode_counts, seg_steps, shapes, spectrum):
    sources, _, bins_here, modes_here = excitation.shape
    all_modes = coupling.shape[-1]
    columns = sources * 2 * bins_here
    first_mode = lax.axis_index("mode") * modes_here
    mode_number = first_mode + jnp.arange(modes_here, dtype=jnp.int32)
    living = (mode_number[None, :] < mode_counts[:, None]).astype(jnp.float32)
    amplitude = (
        (excitation.astype(jnp.float32) * living).astype(jnp.bfloat16).reshape(columns, modes_here)
    )
    for segment in range(coupling.shape[0]):
        stacked = coupling[segment, 0].reshape(2 * modes_here, all_modes)

        def add_portion(running, portion, offset, stacked=stacked):
            return lax.dot_general(
                portion, stacked, (((1,), (1,)), ((), ())), preferred_element_type=jnp.float32
            )

        product = add_portion(
            jnp.zeros((columns, 2 * modes_here), jnp.float32),
            lax.all_gather(amplitude, "mode", axis=1, tiled=True),
            jnp.int32(0),
        )
        product = product.reshape(sources, 2, bins_here, 2, modes_here)
        coupled_real = product[:, 0, :, 0] - product[:, 1, :, 1]
        coupled_imaginary = product[:, 1, :, 0] + product[:, 0, :, 1]
        angles = wavenumber * seg_steps[segment].astype(jnp.float32)
        factor_real = living * jnp.cos(angles)
        factor_imaginary = living * jnp.sin(angles)
        amplitude = jnp.stack(
            [
                coupled_real * factor_real - coupled_imaginary * factor_imaginary,
                coupled_real * factor_imaginary + coupled_imaginary * factor_real,
            ],
            axis=1,
        )
        amplitude = amplitude.astype(jnp.bfloat16).reshape(columns, modes_here)
    mode_shapes = shapes[0]
    field = lax.dot_general(
        lax.all_to_all(
            amplitude.reshape(sources, 2, bins_here, modes_here),
            "mode",
            split_axis=0,
            concat_axis=3,
            tiled=True,
        ),
        mode_shapes,
        (((3,), (0,)), ((), ())),
        preferred_element_type=jnp.float32,
    )
    weight_real = spectrum[0][None, :, None]
    weight_imaginary = spectrum[1][None, :, None]
    weighted = jnp.stack(
        [
            weight_real * field[:, 0] - weight_imaginary * field[:, 1],
            weight_real * field[:, 1] + weight_imaginary * field[:, 0],
        ],
        axis=1,
    ).astype(jnp.bfloat16)
    all_bins = bins_here * lax.axis_size("freq")
    offset_bin = all_bins // 16
    table = make_table(all_bins, offset_bin)
    summed = lax.dot_general(
        lax.all_to_all(weighted, "freq", split_axis=3, concat_axis=2, tiled=True),
        table,
        (((1, 2), (0, 1)), ((), ())),
        preferred_element_type=jnp.float32,
    )
    return summed * (1.0 / math.sqrt(all_bins))


def solution(mesh):
    in_specs = (
        P(None, None, "freq", "mode"),
        P(None, "freq", None, "mode", None),
        P("freq", "mode"),
        P("freq"),
        P(),
        P("freq", None, None),
        P(None, "freq"),
    )
    out_specs = P("mode", "freq", None)
    return jax.shard_map(shards, mesh=mesh, in_specs=in_specs, out_specs=out_specs, check_vma=False)
```

profile of v0, /device:TPU:1, one launch (start us, length us, event | category | flops | bytes accessed | tf_op | source)
XLA Modules:
  0.0 331.4 jit_solution(11354796678249846747)
XLA Ops:
  6.5 0.9 compare_convert_fusion
  7.4 2.0 multiply_convert_fusion
  9.5 1.4 fusion.30
  12.9 1.1 compare_select_fusion.5
  14.0 58.2 %all-gather.4.cloned.1.call-done = bf16[1024,2048]{1,0:T(8,128)(2,1)} async-done(((bf16[1024,256]{1,0:T(8,128)(2,1)}), bf16[1024,2048]{1,0:T(8,128)(2,1)}) %all-gather.4.cloned.1.call-update) | async-done | bytes 4194320 | tf_op jit(solution)/shard_map/all_gather | solution.py:38
  72.1 5.2 %fusion.15 = f32[16,2,32,2,256]{4,2,3,1,0:T(8,128)S(1)} fusion(bf16[16,2,32,2048,1]{3,2,4,1,0:T(8,128)(2,1)} %bitcast.183, bf16[3,1,2,256,2048]{4,3,2,1,0:T(8,128)(2,1)} %param.8), kind=kOutput, calls=%fused_computation.21 | convolution fusion | flops 2147483648 | bytes 8388608 | tf_op jit(solution)/shard_map/dot_general | solution.py:32
  77.4 0.3 subtract_convert_fusion.2
  77.7 0.1 pad_maximum_fusion
  77.7 0.8 copy.29
  78.6 61.2 %all-gather.6.cloned.1.call-done = bf16[1024,2048]{1,0:T(8,128)(2,1)} async-done(((bf16[1024,256]{1,0:T(8,128)(2,1)}), bf16[1024,2048]{1,0:T(8,128)(2,1)}) %all-gather.6.cloned.1.call-update) | async-done | bytes 4194320 | tf_op jit(solution)/shard_map/all_gather | solution.py:38
  139.9 5.2 %fusion.13 = f32[16,2,32,2,256]{4,2,3,1,0:T(8,128)S(1)} fusion(bf16[16,2,32,2048,1]{3,2,4,1,0:T(8,128)(2,1)} %bitcast.184, bf16[3,1,2,256,2048]{4,3,2,1,0:T(8,128)(2,1)} %param.8), kind=kOutput, calls=%fused_computation.19 | convolution fusion | flops 2147483648 | bytes 8388608 | tf_op jit(solution)/shard_map/dot_general | solution.py:32
  145.1 0.3 subtract_convert_fusion.1
  145.4 0.8 copy.32
  146.3 61.3 %all-gather.8.cloned.1.call-done = bf16[1024,2048]{1,0:T(8,128)(2,1)} async-done(((bf16[1024,256]{1,0:T(8,128)(2,1)}), bf16[1024,2048]{1,0:T(8,128)(2,1)}) %all-gather.8.cloned.1.call-update) | async-done | bytes 4194320 | tf_op jit(solution)/shard_map/all_gather | solution.py:38
  207.6 5.2 %fusion.11 = f32[16,2,32,2,256]{4,2,3,1,0:T(8,128)S(1)} fusion(bf16[16,2,32,2048,1]{3,2,4,1,0:T(8,128)(2,1)} %bitcast.185, bf16[3,1,2,256,2048]{4,3,2,1,0:T(8,128)(2,1)} %param.8), kind=kOutput, calls=%fused_computation.17 | convolution fusion | flops 2147483648 | bytes 8388608 | tf_op jit(solution)/shard_map/dot_general | solution.py:32
  212.8 0.3 subtract_convert_fusion
  213.1 0.8 copy.35
  214.0 3.5 %all-to-all-start = ((bf16[16,2,32,256]{3,2,1,0:T(8,128)(2,1)}), bf16[16,2,32,256]{3,2,1,0:T(8,128)(2,1)S(1)}, u32[]{:S(2)}, u32[]{:S(2)}) async-start(bf16[16,2,32,256]{3,2,1,0:T(8,128)(2,1)} %copy.35), calls=%async_computation | async-start | bytes 1048576 | tf_op jit(solution)/shard_map/all_to_all | solution.py:57
  217.5 12.2 %all-to-all-done = bf16[16,2,32,256]{3,2,1,0:T(8,128)(2,1)S(1)} async-done(((bf16[16,2,32,256]{3,2,1,0:T(8,128)(2,1)}), bf16[16,2,32,256]{3,2,1,0:T(8,128)(2,1)S(1)}, u32[]{:S(2)}, u32[]{:S(2)}) %all-to-all-start) | async-done | bytes 524320 | tf_op jit(solution)/shard_map/all_to_all | solution.py:57
  229.7 0.3 copy.55
  230.0 0.2 all_to_all.29
  230.3 0.5 fusion.9
  230.7 0.1 subtract_convert_fusion.3
  230.9 0.4 copy.37
  231.3 1.2 reshape.388
  232.5 13.2 %all-to-all-start.1 = ((bf16[32,2,1024]{2,1,0:T(2,128)(2,1)}), bf16[32,2,1024]{2,1,0:T(2,128)(2,1)S(1)}, u32[]{:S(2)}, u32[]{:S(2)}) async-start(bf16[32,2,1024]{2,1,0:T(2,128)(2,1)} %reshape.388), calls=%async_computation.1 | async-start | bytes 262144 | tf_op jit(solution)/shard_map/all_to_all | solution.py:81
  245.7 70.0 %cosine_convert_fusion = (bf16[1,1024,4096]{2,1,0:T(8,128)(2,1)}, bf16[1,1024,4096]{2,1,0:T(8,128)(2,1)}) fusion(s32[1024]{0:T(1024)S(1)} %iota_add_fusion), kind=kLoop, calls=%fused_computation.8 | loop fusion | flops 71303168 | bytes 16781312 | tf_op jit(solution)/shard_map/convert
  315.7 0.3 reshape.389
  315.9 0.1 copy.38
  316.0 0.1 copy.39
  316.2 0.5 all_to_all.33
  316.7 8.2 %fusion.8 = f32[2,16,4096]{2,1,0:T(8,128)} fusion(bf16[2,2,1024,16]{2,3,1,0:T(8,128)(2,1)S(1)} %all_to_all.33, bf16[1,1024,4096]{2,1,0:T(8,128)(2,1)} %get-tuple-element.20, bf16[1,1024,4096]{2,1,0:T(8,128)(2,1)} %get-tuple-element.19), kind=kOutput, calls=%fused_computation.14 | convolution fusion | flops 545390592 | bytes 17432576 | tf_op jit(solution)/shard_map/dot_general | solution.py:80
  (17 shorter events, 0.3 us)
Async XLA Ops:
  6.5 223.7 %copy-start = (bf16[1,2048,512]{2,1,0:T(8,128)(2,1)S(1)}, bf16[1,2048,512]{2,1,0:T(8,128)(2,1)}, u32[]{:S(2)}) copy-start(bf16[1,2048,512]{2,1,0:T(8,128)(2,1)} %param.12) | copy-start | bytes 6291460
  6.5 65.6 %all-gather.4.cloned.1.call-start = ((), (), s32[]{:S(2)}) async-start(), calls=%async_computation.2 | async-start | bytes 4718592 | tf_op jit(solution)/shard_map/all_gather | solution.py:38
  9.4 130.5 %all-gather.6.cloned.1.call-start = ((), (), s32[]{:S(2)}) async-start(), calls=%async_computation.3 | async-start | bytes 4718592 | tf_op jit(solution)/shard_map/all_gather | solution.py:38
  78.6 129.0 %all-gather.8.cloned.1.call-start = ((), (), s32[]{:S(2)}) async-start(), calls=%async_computation.4 | async-start | bytes 4718592 | tf_op jit(solution)/shard_map/all_gather | solution.py:38
  207.6 9.9 %copy-start.1 = (f32[2,32]{1,0:T(2,128)S(1)}, f32[2,32]{1,0:T(2,128)}, u32[]{:S(2)}) copy-start(f32[2,32]{1,0:T(2,128)} %param.13) | copy-start | bytes 772
  214.0 15.7 %all-to-all-start = ((bf16[16,2,32,256]{3,2,1,0:T(8,128)(2,1)}), bf16[16,2,32,256]{3,2,1,0:T(8,128)(2,1)S(1)}, u32[]{:S(2)}, u32[]{:S(2)}) async-start(bf16[16,2,32,256]{3,2,1,0:T(8,128)(2,1)} %copy.35), calls=%async_computation | async-start | bytes 1048576 | tf_op jit(solution)/shard_map/all_to_all | solution.py:57
  232.5 83.2 %all-to-all-start.1 = ((bf16[32,2,1024]{2,1,0:T(2,128)(2,1)}), bf16[32,2,1024]{2,1,0:T(2,128)(2,1)S(1)}, u32[]{:S(2)}, u32[]{:S(2)}) async-start(bf16[32,2,1024]{2,1,0:T(2,128)(2,1)} %reshape.388), calls=%async_computation.1 | async-start | bytes 262144 | tf_op jit(solution)/shard_map/all_to_all | solution.py:81
Sparse Core Ops, SparseCore 0:
  9.5 62.5 all-gather.3
  78.7 61.1 all-gather.5
  146.4 61.1 all-gather.7
where the time goes:
time: 332 us; the launch traced here: 331 us
  waiting for transfers between devices  193 us (58%)
  other arithmetic  75.1 us (23%)
  matrix products  24.4 us (7%)
  starting transfers between devices  16.8 us (5%)
  between operations  15.3 us (5%)
  local copies, waits for them, and re-layouts  7.04 us (2%)
    all_gather x3, waiting for transfers between devices, shards(): lax.all_gather(amplitude, 'mode', axis=1, tiled=True)  181 us
    another operation x5, other arithmetic  70.9 us
    dot_general x3, matrix products, add_portion(): lax.dot_general(portion, stacked, (((1,), (1,)), ((), ())), preferred_ele...  15.7 us
    all_to_all x1, starting transfers between devices, shards(): lax.all_to_all(weighted, 'freq', split_axis=3, concat_axis=2, tiled=True)  13.2 us
    all_to_all x1, waiting for transfers between devices, shards(): lax.all_to_all(amplitude.reshape(sources, 2, bins_here, modes_here), 'mod...  12.2 us
    dot_general x1, matrix products, shards(): lax.dot_general(lax.all_to_all(weighted, 'freq', split_axis=3, concat_axi...  8.21 us
  transfers between devices with their start and end apart: 5, of which 4 were waited for; matrix products, arithmetic and copies ran while one was open for 22% of the time, Pallas kernels for 0%

commit v1 on v0

--- a/solution.py
+++ b/solution.py
@@ -35,7 +35,9 @@
 
         product = add_portion(
             jnp.zeros((columns, 2 * modes_here), jnp.float32),
-            lax.all_gather(amplitude, "mode", axis=1, tiled=True),
+            jnp.concatenate(
+                lax.all_to_all(jnp.stack([amplitude] * lax.axis_size("mode")), "mode", 0, 0), axis=1
+            ),
             jnp.int32(0),
         )
         product = product.reshape(sources, 2, bins_here, 2, modes_here)

time: 332 us -> 473 us (1.42)
  blocking collectives: 0 us -> 196 us
  waiting for transfers between devices: 193 us -> 109 us
  local copies, waits for them, and re-layouts: 7.04 us -> 45.1 us
  between operations: 15.3 us -> 2.18 us
  starting transfers between devices: 16.8 us -> 22 us
    all_to_all x0 -> x2, blocking collectives: none -> 196 us  [shards(): lax.all_to_all(jnp.stack([amplitude] * lax.axis_size('mode')), 'mode', 0, 0)]
    all_gather x3 -> x0, waiting for transfers between devices: 181 us -> none  [shards(): lax.all_gather(amplitude, 'mode', axis=1, tiled=True)]
    all_to_all x0 -> x1, waiting for transfers between devices: none -> 93.9 us  [shards(): lax.all_to_all(jnp.stack([amplitude] * lax.axis_size('mode')), 'mode', 0, 0)]
    dot_general x0 -> x3, local copies, waits for them, and re-layouts: none -> 22.3 us  [add_portion(): lax.dot_general(portion, stacked, (((1,), (1,)), ((), ())), preferred_ele...]
    reshape x0 -> x3, local copies, waits for them, and re-layouts: none -> 15.3 us  [shards(): jnp.concatenate(lax.all_to_all(jnp.stack([amplitude] * lax.axis_size('mod...]
    all_to_all x0 -> x1, starting transfers between devices: none -> 9.13 us  [shards(): lax.all_to_all(jnp.stack([amplitude] * lax.axis_size('mode')), 'mode', 0, 0)]
  transfers between devices with their start and end apart: 5 -> 3, of which waited for: 4 -> 2; matrix products, arithmetic and copies ran while one was open for 22% -> 15% of each run, Pallas kernels for 0% -> 0%
where the time goes in v1:
time: 473 us; the launch traced here: 472 us
  blocking collectives  196 us (41%)
  waiting for transfers between devices  109 us (23%)
  other arithmetic  73.5 us (16%)
  local copies, waits for them, and re-layouts  45.1 us (10%)
  matrix products  24.3 us (5%)
  starting transfers between devices  22 us (5%)
    all_to_all x2, blocking collectives, shards(): lax.all_to_all(jnp.stack([amplitude] * lax.axis_size('mode')), 'mode', 0, 0)  196 us
    all_to_all x1, waiting for transfers between devices, shards(): lax.all_to_all(jnp.stack([amplitude] * lax.axis_size('mode')), 'mode', 0, 0)  93.9 us
    another operation x5, other arithmetic  70.9 us
    dot_general x3, local copies, waits for them, and re-layouts, add_portion(): lax.dot_general(portion, stacked, (((1,), (1,)), ((), ())), preferred_ele...  22.3 us
    dot_general x3, matrix products, add_portion(): lax.dot_general(portion, stacked, (((1,), (1,)), ((), ())), preferred_ele...  15.7 us
    reshape x3, local copies, waits for them, and re-layouts, shards(): jnp.concatenate(lax.all_to_all(jnp.stack([amplitude] * lax.axis_size('mod...  15.3 us
    all_to_all x1, waiting for transfers between devices, shards(): lax.all_to_all(amplitude.reshape(sources, 2, bins_here, modes_here), 'mod...  15.3 us
  transfers between devices with their start and end apart: 3, of which 2 were waited for; matrix products, arithmetic and copies ran while one was open for 15% of the time, Pallas kernels for 0%

profile of v1, /device:TPU:1, one launch (start us, length us, event | category | flops | bytes accessed | tf_op | source)
XLA Modules:
  0.0 472.1 jit_solution(10030179837268180067)
XLA Ops:
  0.0 0.9 compare_convert_fusion
  0.9 1.2 multiply_convert_fusion
  2.0 2.3 stack.39
  4.3 9.1 %all-to-all-start = ((bf16[8,1024,256]{2,1,0:T(8,128)(2,1)}), bf16[8,1024,256]{2,1,0:T(8,128)(2,1)}, u32[]{:S(2)}, u32[]{:S(2)}) async-start(bf16[8,1024,256]{2,1,0:T(8,128)(2,1)} %stack.39), calls=%async_computation | async-start | bytes 8388608 | tf_op jit(solution)/shard_map/all_to_all | solution.py:39
  13.5 0.7 fusion.33
  16.0 0.4 compare_select_fusion.5
  16.4 93.9 %all-to-all-done = bf16[8,1024,256]{2,1,0:T(8,128)(2,1)} async-done(((bf16[8,1024,256]{2,1,0:T(8,128)(2,1)}), bf16[8,1024,256]{2,1,0:T(8,128)(2,1)}, u32[]{:S(2)}, u32[]{:S(2)}) %all-to-all-start) | async-done | bytes 4194336 | tf_op jit(solution)/shard_map/all_to_all | solution.py:39
  110.3 6.5 %copy.27 = bf16[1024,8,256]{2,1,0:T(8,128)(2,1)} copy(bf16[1024,8,256]{2,0,1:T(8,128)(2,1)} %bitcast.2) | data formatting | bytes 8388608 | tf_op jit(solution)/shard_map/reshape | solution.py:38
  116.8 7.4 %reshape.397 = bf16[16,2,32,2048,1]{3,2,1,0,4:T(8,128)(2,1)} reshape(bf16[1024,8,256]{2,1,0:T(8,128)(2,1)} %copy.27) | data formatting | bytes 8388608 | tf_op jit(solution)/shard_map/dot_general | solution.py:32
  124.2 5.2 %fusion.13 = f32[16,2,32,2,256]{4,2,3,1,0:T(8,128)S(1)} fusion(bf16[16,2,32,2048,1]{3,2,1,0,4:T(8,128)(2,1)} %reshape.397, bf16[3,1,2,256,2048]{4,3,2,1,0:T(8,128)(2,1)} %param.8), kind=kOutput, calls=%fused_computation.19 | convolution fusion | flops 2147483648 | bytes 8388608 | tf_op jit(solution)/shard_map/dot_general | solution.py:32
  129.5 0.3 subtract_convert_fusion.2
  130.1 98.6 %all_to_all.51 = bf16[8,1024,256]{2,1,0:T(8,128)(2,1)S(1)} all-to-all(bf16[8,1024,256]{2,1,0:T(8,128)(2,1)S(1)} %stack.41), channel_id=1, replica_groups=mesh['freq'=32,'mode'=8] {'mode'}, dimensions={0} | all-to-all | bytes 8388608 | tf_op jit(solution)/shard_map/all_to_all | solution.py:39
  228.7 4.4 copy.31
  233.1 7.5 %reshape.399 = bf16[16,2,32,2048,1]{3,2,1,0,4:T(8,128)(2,1)} reshape(bf16[1024,8,256]{2,1,0:T(8,128)(2,1)} %copy.31) | data formatting | bytes 8388608 | tf_op jit(solution)/shard_map/dot_general | solution.py:32
  240.6 5.2 %fusion.11 = f32[16,2,32,2,256]{4,2,3,1,0:T(8,128)S(1)} fusion(bf16[16,2,32,2048,1]{3,2,1,0,4:T(8,128)(2,1)} %reshape.399, bf16[3,1,2,256,2048]{4,3,2,1,0:T(8,128)(2,1)} %param.8), kind=kOutput, calls=%fused_computation.17 | convolution fusion | flops 2147483648 | bytes 8388608 | tf_op jit(solution)/shard_map/dot_general | solution.py:32
  245.8 0.3 subtract_convert_fusion.1
  246.5 97.3 %all_to_all.52 = bf16[8,1024,256]{2,1,0:T(8,128)(2,1)S(1)} all-to-all(bf16[8,1024,256]{2,1,0:T(8,128)(2,1)S(1)} %stack.43), channel_id=1, replica_groups=mesh['freq'=32,'mode'=8] {'mode'}, dimensions={0} | all-to-all | bytes 8388608 | tf_op jit(solution)/shard_map/all_to_all | solution.py:39
  343.7 4.4 copy.35
  348.1 7.5 %reshape.401 = bf16[16,2,32,2048,1]{3,2,1,0,4:T(8,128)(2,1)} reshape(bf16[1024,8,256]{2,1,0:T(8,128)(2,1)} %copy.35) | data formatting | bytes 8388608 | tf_op jit(solution)/shard_map/dot_general | solution.py:32
  355.5 5.2 %fusion.9 = f32[16,2,32,2,256]{4,2,3,1,0:T(8,128)S(1)} fusion(bf16[16,2,32,2048,1]{3,2,1,0,4:T(8,128)(2,1)} %reshape.401, bf16[3,1,2,256,2048]{4,3,2,1,0:T(8,128)(2,1)} %param.8), kind=kOutput, calls=%fused_computation.15 | convolution fusion | flops 2147483648 | bytes 8388608 | tf_op jit(solution)/shard_map/dot_general | solution.py:32
  360.8 0.3 subtract_convert_fusion
  361.1 0.8 copy.38
  362.0 3.7 all-to-all-start.3
  365.7 15.3 %all-to-all-done.3 = bf16[16,2,32,256]{3,2,1,0:T(8,128)(2,1)S(1)} async-done(((bf16[16,2,32,256]{3,2,1,0:T(8,128)(2,1)}), bf16[16,2,32,256]{3,2,1,0:T(8,128)(2,1)S(1)}, u32[]{:S(2)}, u32[]{:S(2)}) %all-to-all-start.3) | async-done | bytes 524320 | tf_op jit(solution)/shard_map/all_to_all | solution.py:59
  381.0 0.3 copy.58
  381.6 0.4 fusion.15
  382.2 0.4 copy.40
  382.5 1.2 reshape.409
  383.7 9.1 %all-to-all-start.4 = ((bf16[32,2,1024]{2,1,0:T(2,128)(2,1)}), bf16[32,2,1024]{2,1,0:T(2,128)(2,1)S(1)}, u32[]{:S(2)}, u32[]{:S(2)}) async-start(bf16[32,2,1024]{2,1,0:T(2,128)(2,1)} %reshape.409), calls=%async_computation.4 | async-start | bytes 262144 | tf_op jit(solution)/shard_map/all_to_all | solution.py:83
  392.9 70.0 %cosine_convert_fusion = (bf16[1,1024,4096]{2,1,0:T(8,128)(2,1)}, bf16[1,1024,4096]{2,1,0:T(8,128)(2,1)}) fusion(s32[1024]{0:T(1024)S(1)} %iota_add_fusion), kind=kLoop, calls=%fused_computation.8 | loop fusion | flops 71303168 | bytes 16781312 | tf_op jit(solution)/shard_map/convert
  463.4 0.5 all_to_all.45
  463.9 8.2 %fusion.8 = f32[2,16,4096]{2,1,0:T(8,128)} fusion(bf16[2,2,1024,16]{2,3,1,0:T(8,128)(2,1)S(1)} %all_to_all.45, bf16[1,1024,4096]{2,1,0:T(8,128)(2,1)} %get-tuple-element.20, bf16[1,1024,4096]{2,1,0:T(8,128)(2,1)} %get-tuple-element.19), kind=kOutput, calls=%fused_computation.14 | convolution fusion | flops 545390592 | bytes 17432576 | tf_op jit(solution)/shard_map/dot_general | solution.py:82
  (27 shorter events, 1.6 us)
Async XLA Ops:
  0.0 381.6 %copy-start = (bf16[1,2048,512]{2,1,0:T(8,128)(2,1)S(1)}, bf16[1,2048,512]{2,1,0:T(8,128)(2,1)}, u32[]{:S(2)}) copy-start(bf16[1,2048,512]{2,1,0:T(8,128)(2,1)} %param.12) | copy-start | bytes 6291460
  4.3 9.1 %copy-start.2 = (s32[3]{0:T(128)S(1)}, s32[3]{0:T(128)}, u32[]{:S(2)}) copy-start(s32[3]{0:T(128)} %param.11) | copy-start | bytes 40
  4.3 11.7 %copy-start.1 = (f32[32,256]{1,0:T(8,128)S(1)}, f32[32,256]{1,0:T(8,128)}, u32[]{:S(2)}) copy-start(f32[32,256]{1,0:T(8,128)} %param.9) | copy-start | bytes 98308
  4.3 11.7 %copy-start.3 = (s32[32]{0:T(128)S(1)}, s32[32]{0:T(128)}, u32[]{:S(2)}) copy-start(s32[32]{0:T(128)} %param.10) | copy-start | bytes 388
  4.3 106.0 %all-to-all-start = ((bf16[8,1024,256]{2,1,0:T(8,128)(2,1)}), bf16[8,1024,256]{2,1,0:T(8,128)(2,1)}, u32[]{:S(2)}, u32[]{:S(2)}) async-start(bf16[8,1024,256]{2,1,0:T(8,128)(2,1)} %stack.39), calls=%async_computation | async-start | bytes 8388608 | tf_op jit(solution)/shard_map/all_to_all | solution.py:39
  360.8 4.9 %copy-start.4 = (f32[2,32]{1,0:T(2,128)S(1)}, f32[2,32]{1,0:T(2,128)}, u32[]{:S(2)}) copy-start(f32[2,32]{1,0:T(2,128)} %param.13) | copy-start | bytes 772
  362.0 19.0 %all-to-all-start.3 = ((bf16[16,2,32,256]{3,2,1,0:T(8,128)(2,1)}), bf16[16,2,32,256]{3,2,1,0:T(8,128)(2,1)S(1)}, u32[]{:S(2)}, u32[]{:S(2)}) async-start(bf16[16,2,32,256]{3,2,1,0:T(8,128)(2,1)} %copy.38), calls=%async_computation.3 | async-start | bytes 1048576 | tf_op jit(solution)/shard_map/all_to_all | solution.py:59
  383.7 79.2 %all-to-all-start.4 = ((bf16[32,2,1024]{2,1,0:T(2,128)(2,1)}), bf16[32,2,1024]{2,1,0:T(2,128)(2,1)S(1)}, u32[]{:S(2)}, u32[]{:S(2)}) async-start(bf16[32,2,1024]{2,1,0:T(2,128)(2,1)} %reshape.409), calls=%async_computation.4 | async-start | bytes 262144 | tf_op jit(solution)/shard_map/all_to_all | solution.py:83
